TPU v7x, 32 devices: a whole 2x2x4 slice. The times are simulated.
32 devices in a mesh: grp: 8 (over z, y), ctx: 2 (over x), wsh: 2 (over core).
Axes of the slice: x: 2, y: 2, z: 4, core: 2. Of those that a mesh axis runs over, the one named last changes fastest.
Arguments:
- tokens: bfloat16 [16, 1024, 768], P(('grp', 'wsh'), 'ctx'), may hold values from -6 to 6
- lengths: int32 [16], P(('grp', 'wsh')), may hold values from 256 to 1024, as said below
- query_weight: bfloat16 [768, 768], P('wsh'), may hold values from -0.21875 to 0.21875
- key_weight: bfloat16 [768, 768], P('wsh'), may hold values from -0.21875 to 0.21875
- value_weight: bfloat16 [768, 768], P('wsh'), may hold values from -0.21875 to 0.21875
- output_weight: bfloat16 [768, 768], P('wsh'), may hold values from -3.5 to 3.5
- gate_weight: bfloat16 [768, 2048], P('wsh'), may hold values from -0.21875 to 0.21875
- up_weight: bfloat16 [768, 2048], P('wsh'), may hold values from -0.21875 to 0.21875
- down_weight: bfloat16 [2048, 768], P('wsh'), may hold values from -0.125 to 0.125
- attn_gain: bfloat16 [768], P('wsh'), may hold values from 0.5 to 1.5
- ffn_gain: bfloat16 [768], P('wsh'), may hold values from 0.5 to 1.5
- out_grad: bfloat16 [16, 1024, 768], P(('grp', 'wsh'), 'ctx'), may hold values from -6 to 6
Outputs:
- output: bfloat16 [16, 1024, 768], P(('grp', 'wsh'), 'ctx')
- input_grad: bfloat16 [16, 1024, 768], P(('grp', 'wsh'), 'ctx')
- query_grad: float32 [768, 768], P('wsh')
- key_grad: float32 [768, 768], P('wsh')
- value_grad: float32 [768, 768], P('wsh')
- output_weight_grad: float32 [768, 768], P('wsh')
- gate_grad: float32 [768, 2048], P('wsh')
- up_grad: float32 [768, 2048], P('wsh')
- down_grad: float32 [2048, 768], P('wsh')
- attn_gain_grad: float32 [768], P('wsh')
- ffn_gain_grad: float32 [768], P('wsh')
Inputs may be any that keep to these rules, and one draw needn't show every extreme that they name: `lengths`: valid positions of each sequence; in every draw some sequence has exactly 1024 and some other exactly 256.
All inputs are finite; a program needn't handle non-finite values.
Results may differ from a plain program's by a relative error of at most 0.02.
Values may be sent and summed in bfloat16 or wider, within the bound.
No kernel may reach another device: no remote copies, remote signals or barrier semaphores. Data moves between devices by JAX's collectives and lax.ppermute only.
A program may use at most 320 MiB of HBM per device.

v0:
```python
import jax
import jax.numpy as jnp
from jax import lax
from jax.sharding import PartitionSpec as P

D = 768
HEADS = 12
HEAD_DIM = 64


epsilon = 1e-06
floor_score = -1e30


def rms_scale(values):
    return lax.rsqrt(jnp.mean(values * values, axis=-1, keepdims=True) + epsilon)


def norm_backward(grad_normed, values, scale_rows, gain_vec):
    scaled_grad = grad_normed * gain_vec
    grad_gain = jnp.sum(grad_normed * values * scale_rows, axis=0)
    cubed = scale_rows * scale_rows * scale_rows
    grad_values = scale_rows * scaled_grad - values * cubed * jnp.mean(
        scaled_grad * values, axis=-1, keepdims=True
    )
    return (grad_values, grad_gain)


def gated_mix(gate_rows, up_rows):
    return jax.nn.gelu(gate_rows, approximate=True) * up_rows


def on_device(
    tokens,
    lengths,
    query_weight,
    key_weight,
    value_weight,
    output_weight,
    gate_weight,
    up_weight,
    down_weight,
    attn_gain,
    ffn_gain,
    out_grad,
):
    gathered = (
        lax.all_gather(query_weight, "wsh", axis=0, tiled=True),
        lax.all_gather(key_weight, "wsh", axis=0, tiled=True),
        lax.all_gather(value_weight, "wsh", axis=0, tiled=True),
        lax.all_gather(output_weight, "wsh", axis=0, tiled=True),
        lax.all_gather(gate_weight, "wsh", axis=0, tiled=True),
        lax.all_gather(up_weight, "wsh", axis=0, tiled=True),
        lax.all_gather(down_weight, "wsh", axis=0, tiled=True),
        lax.all_gather(attn_gain, "wsh", axis=0, tiled=True),
        lax.all_gather(ffn_gain, "wsh", axis=0, tiled=True),
    )
    (
        query_full,
        key_full,
        value_full,
        output_full,
        gate_full,
        up_full,
        down_full,
        gain_attn,
        gain_ffn,
    ) = gathered
    gain_first = gain_attn.astype(jnp.float32)
    gain_second = gain_ffn.astype(jnp.float32)
    shard_rows = tokens.shape[1]
    cycle_size = lax.axis_size("ctx")
    whole_rows = shard_rows * cycle_size
    length = lengths[0]
    own_start = lax.axis_index("ctx") * shard_rows
    row_live = own_start + jnp.arange(shard_rows, dtype=jnp.int32) < length
    factor = HEAD_DIM ** (-0.5)
    block_rows = min(whole_rows, max(shard_rows, 512))
    block_count = whole_rows // block_rows
    block_starts = jnp.arange(block_count, dtype=jnp.int32) * block_rows
    row_input = tokens[0].astype(jnp.float32)
    scale_first = rms_scale(row_input)
    normed_first = (row_input * scale_first * gain_first).astype(jnp.bfloat16)
    query_rows = jnp.dot(normed_first, query_full, preferred_element_type=jnp.float32).astype(
        jnp.bfloat16
    )
    key_rows = jnp.dot(normed_first, key_full, preferred_element_type=jnp.float32).astype(
        jnp.bfloat16
    )
    value_rows = jnp.dot(normed_first, value_full, preferred_element_type=jnp.float32).astype(
        jnp.bfloat16
    )
    query_heads = query_rows.reshape(shard_rows, HEADS, HEAD_DIM)

    def piece_scores(key_piece, begin):
        piece_rows = key_piece.shape[0]
        key_heads = key_piece.reshape(piece_rows, HEADS, HEAD_DIM)
        scores = (
            jnp.einsum("qhd,khd->hqk", query_heads, key_heads, preferred_element_type=jnp.float32)
            * factor
        )
        key_live = begin + jnp.arange(piece_rows, dtype=jnp.int32) < length
        return (jnp.where(key_live[None, None, :], scores, floor_score), key_live)

    row_max = jnp.full((HEADS, shard_rows), floor_score, jnp.float32)
    key_piece = lax.all_gather(key_rows, "ctx", axis=0, tiled=True)
    value_piece = lax.all_gather(value_rows, "ctx", axis=0, tiled=True)
    scores, key_live = piece_scores(key_piece, jnp.int32(0))
    new_max = jnp.maximum(row_max, jnp.max(scores, axis=-1))
    weights = jnp.where(key_live[None, None, :], jnp.exp(scores - new_max[:, :, None]), 0.0)
    row_total = jnp.sum(weights, axis=-1)
    value_heads = value_piece.reshape(value_piece.shape[0], HEADS, HEAD_DIM)
    running = jnp.einsum(
        "hqk,khd->qhd",
        weights.astype(jnp.bfloat16),
        value_heads,
        preferred_element_type=jnp.float32,
    )
    final_state = (new_max, row_total, running)
    row_max, row_total, running = final_state
    attended_heads = running / jnp.transpose(row_total)[:, :, None]
    log_total = row_max + jnp.log(row_total)
    attended = attended_heads.reshape(shard_rows, D).astype(jnp.bfloat16)
    middle = row_input + jnp.dot(attended, output_full, preferred_element_type=jnp.float32)
    scale_second = rms_scale(middle)
    normed_second = (middle * scale_second * gain_second).astype(jnp.bfloat16)
    gate_rows = jnp.dot(normed_second, gate_full, preferred_element_type=jnp.float32)
    up_rows = jnp.dot(normed_second, up_full, preferred_element_type=jnp.float32)
    hidden_wide, mix_pullback = jax.vjp(gated_mix, gate_rows, up_rows)
    hidden = hidden_wide.astype(jnp.bfloat16)
    result = middle + jnp.dot(hidden, down_full, preferred_element_type=jnp.float32)
    output = result.astype(jnp.bfloat16)[None]
    grad_result = out_grad[0].astype(jnp.float32) * row_live[:, None].astype(jnp.float32)
    grad_branch = grad_result.astype(jnp.bfloat16)
    down_term = jnp.einsum("tf,td->fd", hidden, grad_branch, preferred_element_type=jnp.float32)
    grad_hidden = jnp.einsum(
        "td,fd->tf", grad_branch, down_full, preferred_element_type=jnp.float32
    )
    grad_gate, grad_up = mix_pullback(grad_hidden)
    gate_low = grad_gate.astype(jnp.bfloat16)
    up_low = grad_up.astype(jnp.bfloat16)
    gate_term = jnp.einsum("td,tf->df", normed_second, gate_low, preferred_element_type=jnp.float32)
    up_term = jnp.einsum("td,tf->df", normed_second, up_low, preferred_element_type=jnp.float32)
    grad_normed_second = jnp.einsum(
        "tf,df->td", gate_low, gate_full, preferred_element_type=jnp.float32
    ) + jnp.einsum("tf,df->td", up_low, up_full, preferred_element_type=jnp.float32)
    grad_middle_norm, ffn_gain_term = norm_backward(
        grad_normed_second, middle, scale_second, gain_second
    )
    grad_middle = grad_result + grad_middle_norm
    middle_low = grad_middle.astype(jnp.bfloat16)
    output_term = jnp.einsum("td,te->de", attended, middle_low, preferred_element_type=jnp.float32)
    grad_attended = jnp.einsum(
        "te,de->td", middle_low, output_full, preferred_element_type=jnp.float32
    ).astype(jnp.bfloat16)
    grad_heads = grad_attended.reshape(shard_rows, HEADS, HEAD_DIM)
    row_delta = jnp.transpose(jnp.sum(grad_heads.astype(jnp.float32) * attended_heads, axis=-1))
    key_back, value_back = (
        lax.all_gather(key_rows, "ctx", axis=0, tiled=True),
        lax.all_gather(value_rows, "ctx", axis=0, tiled=True),
    )

    def block_grads(key_block, value_block, begin):
        scores, key_live = piece_scores(key_block, begin)
        probs_block = jnp.where(
            key_live[None, None, :], jnp.exp(scores - log_total[:, :, None]), 0.0
        )
        value_heads = value_block.reshape(block_rows, HEADS, HEAD_DIM)
        grad_probs = jnp.einsum(
            "qhd,khd->hqk", grad_heads, value_heads, preferred_element_type=jnp.float32
        )
        grad_scores = (probs_block * (grad_probs - row_delta[:, :, None])).astype(jnp.bfloat16)
        return (probs_block, grad_scores)

    zero_query = jnp.zeros((shard_rows, HEADS, HEAD_DIM), jnp.float32)
    back_inputs = (
        key_back.reshape(block_count, block_rows, D),
        value_back.reshape(block_count, block_rows, D),
        block_starts,
    )

    def back_block(grad_query, element):
        key_block, value_block, begin = element
        probs_block, grad_scores = block_grads(key_block, value_block, begin)
        key_heads = key_block.reshape(block_rows, HEADS, HEAD_DIM)
        grad_query = grad_query + jnp.einsum(
            "hqk,khd->qhd", grad_scores, key_heads, preferred_element_type=jnp.float32
        )
        key_piece_grad = (
            jnp.einsum("hqk,qhd->khd", grad_scores, query_heads, preferred_element_type=jnp.float32)
            * factor
        ).reshape(block_rows, D)
        value_piece_grad = jnp.einsum(
            "hqk,qhd->khd",
            probs_block.astype(jnp.bfloat16),
            grad_heads,
            preferred_element_type=jnp.float32,
        ).reshape(block_rows, D)
        return (grad_query, (key_piece_grad, value_piece_grad))

    query_sum, (key_terms, value_terms) = lax.scan(back_block, zero_query, back_inputs)
    grad_keys, grad_values = (
        lax.psum_scatter(
            key_terms.reshape(whole_rows, D).astype(jnp.bfloat16),
            "ctx",
            scatter_dimension=0,
            tiled=True,
        ).astype(jnp.float32),
        lax.psum_scatter(
            value_terms.reshape(whole_rows, D).astype(jnp.bfloat16),
            "ctx",
            scatter_dimension=0,
            tiled=True,
        ).astype(jnp.float32),
    )
    query_low = (query_sum * factor).reshape(shard_rows, D).astype(jnp.bfloat16)
    key_low = grad_keys.astype(jnp.bfloat16)
    value_low = grad_values.astype(jnp.bfloat16)
    query_term = jnp.einsum(
        "td,te->de", normed_first, query_low, preferred_element_type=jnp.float32
    )
    key_term = jnp.einsum("td,te->de", normed_first, key_low, preferred_element_type=jnp.float32)
    value_term = jnp.einsum(
        "td,te->de", normed_first, value_low, preferred_element_type=jnp.float32
    )
    grad_normed_first = jnp.einsum(
        "te,de->td", query_low, query_full, preferred_element_type=jnp.float32
    )
    grad_normed_first = grad_normed_first + jnp.einsum(
        "te,de->td", key_low, key_full, preferred_element_type=jnp.float32
    )
    grad_normed_first = grad_normed_first + jnp.einsum(
        "te,de->td", value_low, value_full, preferred_element_type=jnp.float32
    )
    grad_rows, attn_gain_term = norm_backward(grad_normed_first, row_input, scale_first, gain_first)
    input_grad = (grad_middle + grad_rows).astype(jnp.bfloat16)[None]
    shards = (
        lax.psum_scatter(
            query_term.astype(jnp.bfloat16), "wsh", scatter_dimension=0, tiled=True
        ).astype(jnp.float32),
        lax.psum_scatter(
            key_term.astype(jnp.bfloat16), "wsh", scatter_dimension=0, tiled=True
        ).astype(jnp.float32),
        lax.psum_scatter(
            value_term.astype(jnp.bfloat16), "wsh", scatter_dimension=0, tiled=True
        ).astype(jnp.float32),
        lax.psum_scatter(
            output_term.astype(jnp.bfloat16), "wsh", scatter_dimension=0, tiled=True
        ).astype(jnp.float32),
        lax.psum_scatter(
            gate_term.astype(jnp.bfloat16), "wsh", scatter_dimension=0, tiled=True
        ).astype(jnp.float32),
        lax.psum_scatter(
            up_term.astype(jnp.bfloat16), "wsh", scatter_dimension=0, tiled=True
        ).astype(jnp.float32),
        lax.psum_scatter(
            down_term.astype(jnp.bfloat16), "wsh", scatter_dimension=0, tiled=True
        ).astype(jnp.float32),
        lax.psum_scatter(
            attn_gain_term.astype(jnp.bfloat16), "wsh", scatter_dimension=0, tiled=True
        ).astype(jnp.float32),
        lax.psum_scatter(
            ffn_gain_term.astype(jnp.bfloat16), "wsh", scatter_dimension=0, tiled=True
        ).astype(jnp.float32),
    )
    totals = lax.psum(
        (
            shards[0],
            shards[1],
            shards[2],
            shards[3],
            shards[4],
            shards[5],
            shards[6],
            shards[7],
            shards[8],
        ),
        ("grp", "ctx"),
    )
    return (
        output,
        input_grad,
        totals[0],
        totals[1],
        totals[2],
        totals[3],
        totals[4],
        totals[5],
        totals[6],
        totals[7],
        totals[8],
    )


def solution(mesh):
    in_specs = (
        P(("grp", "wsh"), "ctx", None),
        P(("grp", "wsh")),
        P("wsh", None),
        P("wsh", None),
        P("wsh", None),
        P("wsh", None),
        P("wsh", None),
        P("wsh", None),
        P("wsh", None),
        P("wsh"),
        P("wsh"),
        P(("grp", "wsh"), "ctx", None),
    )
    out_specs = (
        P(("grp", "wsh"), "ctx", None),
        P(("grp", "wsh"), "ctx", None),
        P("wsh", None),
        P("wsh", None),
        P("wsh", None),
        P("wsh", None),
        P("wsh", None),
        P("wsh", None),
        P("wsh", None),
        P("wsh"),
        P("wsh"),
    )
    return jax.shard_map(
        on_device, mesh=mesh, in_specs=in_specs, out_specs=out_specs, check_vma=False
    )
```

profile of v0, /device:TPU:0, one launch (start us, length us, event | category | flops | bytes accessed | tf_op | source)
XLA Modules:
  0.0 1012.4 jit_solution(11649577749144034470)
XLA Ops:
  12.3 9.2 all-gather.18.cloned.1.call-done
  24.6 8.9 all-gather.12.cloned.1.call-done
  48.8 27.1 %all-gather.20.cloned.1.call-done = bf16[1024,768]{1,0:T(8,128)(2,1)} async-done(((bf16[512,768]{1,0:T(8,128)(2,1)}), bf16[1024,768]{1,0:T(8,128)(2,1)}) %all-gather.20.cloned.1.call-update) | async-done | bytes 1572880 | tf_op jit(solution)/shard_map/all_gather | solution.py:106
  78.6 14.1 %fusion.7 = (f32[12,512]{1,0:T(8,128)S(1)}, f32[12,512,1024]{2,1,0:T(8,128)}) fusion(pred[1024]{0:T(1024)(128)(4,1)S(1)} %iota_compare_fusion, bf16[512,12,64]{0,2,1:T(8,128)(2,1)} %bitcast.3, bf16[1024,12,64]{0,2,1:T(8,128)(2,1)} %bitcast.166), kind=kOutput, calls=%fused_computation.17 | convolution fusion | flops 824174592 | bytes 27550720 | tf_op jit(solution)/shard_map/qhd,khd->hqk/dot_general | solution.py:99
  92.7 11.6 %fusion.8 = f32[12,512]{1,0:T(8,128)S(1)} fusion(f32[12,512,1024]{2,1,0:T(8,128)} %get-tuple-element.202, f32[12,512]{1,0:T(8,128)S(1)} %broadcast_maximum_fusion, pred[1024]{0:T(1024)(128)(4,1)S(1)} %iota_compare_fusion), kind=kLoop, calls=%fused_computation.18 | loop fusion | flops 31451136 | bytes 25216000 | tf_op jit(solution)/shard_map/reduce_sum | solution.py:111
  107.7 13.2 %fusion.62 = (bf16[512,12,64]{0,2,1:T(8,128)(2,1)S(1)}, f32[512,12,64]{0,2,1:T(8,128)}) fusion(f32[512,12]{0,1:T(8,128)S(1)} %bitcast.174, bf16[1024,12,64]{0,2,1:T(8,128)(2,1)} %bitcast.169, f32[12,512,1024]{2,1,0:T(8,128)} %get-tuple-element.202, f32[12,512]{1,0:T(8,128)S(1)} %broadcast_maximum_fusion, pred[1024]{0:T(1024)(128)(4,1)S(1)} %iota_compare_fusion), kind=kOutput, calls=%fused_computation.105 | convolution fusion | flops 837550080 | bytes 29148160 | tf_op jit(solution)/shard_map/hqk,khd->qhd/dot_general | solution.py:113
  124.7 5.9 all-gather.24.cloned.1.call-done
  130.6 5.7 fusion.64
  136.3 9.2 all-gather.26.cloned.1.call-done
  145.5 5.7 fusion.65
  151.2 9.2 all-gather.28.cloned.1.call-done
  160.4 9.0 multiply_convert_fusion.1
  183.1 86.1 %while.15 = (s32[]{:T(128)}, f32[512,12,64]{0,2,1:T(8,128)S(1)}, bf16[2,512,768]{2,1,0:T(8,128)(2,1)}, bf16[2,512,768]{2,1,0:T(8,128)(2,1)}, bf16[2,512,768]{2,1...) while((s32[]{:T(128)}, f32[512,12,64]{0,2,1:T(8,128)S(1)}, ...), condition=%wide.region_7.8_spmd.clone, body=%wide.region_6.7_spmd.clone.sunk | while | flops 2052588544 | bytes 85796552 | solution.py:201
  185.1 7.6 fusion.135
  195.8 10.0 multiply_convert_fusion.6
  209.8 7.8 fusion.136
  217.9 5.8 convolution_multiply_fusion.2
  227.9 7.6 fusion.135
  238.7 10.0 multiply_convert_fusion.6
  252.7 7.8 fusion.136
  260.8 5.8 convolution_multiply_fusion.2
  275.4 21.3 %reduce-scatter.10.cloned.1.call-done = bf16[512,768]{1,0:T(8,128)(2,1)} async-done(((bf16[1024,768]{1,0:T(8,128)(2,1)}), bf16[512,768]{1,0:T(8,128)(2,1)}) %reduce-scatter.10.cloned.1.call-update) | async-done | bytes 786448 | tf_op jit(solution)/shard_map/reduce_scatter | solution.py:203
  299.8 25.3 %reduce-scatter.12.cloned.1.call-done = bf16[512,768]{1,0:T(8,128)(2,1)} async-done(((bf16[1024,768]{1,0:T(8,128)(2,1)}), bf16[512,768]{1,0:T(8,128)(2,1)}) %reduce-scatter.12.cloned.1.call-update) | async-done | bytes 786448 | tf_op jit(solution)/shard_map/reduce_scatter | solution.py:209
  328.3 5.1 convolution_convert_fusion.2
  333.5 5.2 convolution_convert_fusion.1
  339.7 5.2 convolution_convert_fusion
  350.2 4.6 fusion.42
  367.2 7.4 reduce-scatter.18.cloned.1.call-done
  374.6 14.8 %reduce-scatter.22.cloned.1.call-done = bf16[384,2048]{1,0:T(8,128)(2,1)} async-done(((bf16[768,2048]{1,0:T(8,128)(2,1)}), bf16[384,2048]{1,0:T(8,128)(2,1)}) %reduce-scatter.22.cloned.1.call-update) | async-done | bytes 1572880 | tf_op jit(solution)/shard_map/reduce_scatter | solution.py:250
  389.4 14.9 %reduce-scatter.24.cloned.1.call-done = bf16[384,2048]{1,0:T(8,128)(2,1)} async-done(((bf16[768,2048]{1,0:T(8,128)(2,1)}), bf16[384,2048]{1,0:T(8,128)(2,1)}) %reduce-scatter.24.cloned.1.call-update) | async-done | bytes 1572880 | tf_op jit(solution)/shard_map/reduce_scatter | solution.py:253
  404.2 14.8 %reduce-scatter.26.cloned.1.call-done = bf16[1024,768]{1,0:T(8,128)(2,1)} async-done(((bf16[2048,768]{1,0:T(8,128)(2,1)}), bf16[1024,768]{1,0:T(8,128)(2,1)}) %reduce-scatter.26.cloned.1.call-update) | async-done | bytes 1572880 | tf_op jit(solution)/shard_map/reduce_scatter | solution.py:256
  419.0 586.3 %all-reduce.5 = (f32[384,768]{1,0:T(8,128)}, f32[384,768]{1,0:T(8,128)}, f32[384,768]{1,0:T(8,128)}, f32[384,768]{1,0:T(8,128)}, f32[384,2048]{1,0:T(8,128)}, /*...) all-reduce(bf16[384,768]{1,0:T(8,128)(2,1)S(1)} %copy-done.20, ...), channel_id=1, replica_groups=mesh['grp'=8,'ctx'=2,'wsh'=2] {'grp','ctx'}, use_global_device_ids=true, to_apply=%region_12.13 | all-reduce | flops 3539712 | bytes 21239808 | tf_op jit(solution)/shard_map/psum | solution.py:266
  (187 shorter events, 99.4 us)
Async XLA Ops:
  7.2 4.3 copy-start.3
  7.2 14.3 %all-gather.18.cloned.1.call-start = ((), (), s32[]{:S(2)}) async-start(), calls=%async_computation.12 | async-start | bytes 1769472 | tf_op jit(solution)/shard_map/all_gather | solution.py:49
  7.9 25.6 %all-gather.12.cloned.1.call-start = ((), (), s32[]{:S(2)}) async-start(), calls=%async_computation.9 | async-start | bytes 1769472 | tf_op jit(solution)/shard_map/all_gather | solution.py:50
  8.7 36.8 %all-gather.16.cloned.1.call-start = ((), (), s32[]{:S(2)}) async-start(), calls=%async_computation.11 | async-start | bytes 1769472 | tf_op jit(solution)/shard_map/all_gather | solution.py:48
  9.4 66.4 %all-gather.20.cloned.1.call-start = ((), (), s32[]{:S(2)}) async-start(), calls=%async_computation.13 | async-start | bytes 2359296 | tf_op jit(solution)/shard_map/all_gather | solution.py:106
  11.5 34.0 %copy-start.22 = (f32[768]{0:T(1024)}, f32[768]{0:T(1024)S(1)}, u32[]{:S(2)}) copy-start(f32[768]{0:T(1024)S(1)} %reshape.151) | copy-start | bytes 9220
  12.3 33.2 %copy-start.24 = (f32[512]{0:T(512)}, f32[512]{0:T(512)S(1)}, u32[]{:S(2)}) copy-start(f32[512]{0:T(512)S(1)} %get-tuple-element.198) | copy-start | bytes 6148
  24.6 80.5 %all-gather.14.cloned.1.call-start = ((), (), s32[]{:S(2)}) async-start(), calls=%async_computation.10 | async-start | bytes 2359296 | tf_op jit(solution)/shard_map/all_gather | solution.py:107
  36.5 84.4 %all-gather.22.cloned.1.call-start = ((), (), s32[]{:S(2)}) async-start(), calls=%async_computation.14 | async-start | bytes 1769472 | tf_op jit(solution)/shard_map/all_gather | solution.py:51
  37.1 93.5 %all-gather.24.cloned.1.call-start = ((), (), s32[]{:S(2)}) async-start(), calls=%async_computation.15 | async-start | bytes 4718592 | tf_op jit(solution)/shard_map/all_gather | solution.py:52
  37.9 107.6 %all-gather.26.cloned.1.call-start = ((), (), s32[]{:S(2)}) async-start(), calls=%async_computation.16 | async-start | bytes 4718592 | tf_op jit(solution)/shard_map/all_gather | solution.py:53
  38.6 121.8 %all-gather.28.cloned.1.call-start = ((), (), s32[]{:S(2)}) async-start(), calls=%async_computation.17 | async-start | bytes 4718592 | tf_op jit(solution)/shard_map/all_gather | solution.py:54
  39.3 257.4 %reduce-scatter.10.cloned.1.call-start = ((), (), s32[]{:S(2)}) async-start(), calls=%async_computation.18 | async-start | bytes 2359296 | tf_op jit(solution)/shard_map/reduce_scatter | solution.py:203
  41.9 134.0 %copy-start.27 = (f32[512]{0:T(512)}, f32[512]{0:T(512)S(1)}, u32[]{:S(2)}) copy-start(f32[512]{0:T(512)S(1)} %fusion.53) | copy-start | bytes 6148
  124.7 20.8 %copy-start.16 = (bf16[512,768]{1,0:T(8,128)(2,1)}, bf16[512,768]{1,0:T(8,128)(2,1)S(1)}, u32[]{:S(2)}) copy-start(bf16[512,768]{1,0:T(8,128)(2,1)S(1)} %multiply_convert_fusion.4) | copy-start | bytes 2359300
  136.3 24.1 %copy-start.11 = (bf16[1,512,768]{2,1,0:T(8,128)(2,1)S(1)}, bf16[1,512,768]{2,1,0:T(8,128)(2,1)}, u32[]{:S(2)}) copy-start(bf16[1,512,768]{2,1,0:T(8,128)(2,1)} %param.25) | copy-start | bytes 2359300
  160.4 9.1 copy-start.31
  169.4 3.9 copy-start.32
  185.1 9.5 copy-start
  227.9 9.5 copy-start
  269.3 55.8 %reduce-scatter.12.cloned.1.call-start = ((), (), s32[]{:S(2)}) async-start(), calls=%async_computation.19 | async-start | bytes 2359296 | tf_op jit(solution)/shard_map/reduce_scatter | solution.py:209
  270.1 84.7 %reduce-scatter.14.cloned.1.call-start = ((), (), s32[]{:S(2)}) async-start(), calls=%async_computation.20 | async-start | bytes 1769472 | tf_op jit(solution)/shard_map/reduce_scatter | solution.py:238
  273.3 81.6 %reduce-scatter.20.cloned.1.call-start = ((), (), s32[]{:S(2)}) async-start(), calls=%async_computation.23 | async-start | bytes 1769472 | tf_op jit(solution)/shard_map/reduce_scatter | solution.py:247
  275.3 91.9 %reduce-scatter.16.cloned.1.call-start = ((), (), s32[]{:S(2)}) async-start(), calls=%async_computation.21 | async-start | bytes 1769472 | tf_op jit(solution)/shard_map/reduce_scatter | solution.py:241
  299.8 28.5 %copy-start.17 = (bf16[512,768]{1,0:T(8,128)(2,1)S(1)}, bf16[512,768]{1,0:T(8,128)(2,1)}, u32[]{:S(2)}) copy-start(bf16[512,768]{1,0:T(8,128)(2,1)} %copy-done.16) | copy-start | bytes 2359300
  299.8 74.8 %reduce-scatter.18.cloned.1.call-start = ((), (), s32[]{:S(2)}) async-start(), calls=%async_computation.22 | async-start | bytes 1769472 | tf_op jit(solution)/shard_map/reduce_scatter | solution.py:244
  328.2 61.2 %reduce-scatter.22.cloned.1.call-start = ((), (), s32[]{:S(2)}) async-start(), calls=%async_computation.24 | async-start | bytes 4718592 | tf_op jit(solution)/shard_map/reduce_scatter | solution.py:250
  333.4 70.8 %reduce-scatter.24.cloned.1.call-start = ((), (), s32[]{:S(2)}) async-start(), calls=%async_computation.25 | async-start | bytes 4718592 | tf_op jit(solution)/shard_map/reduce_scatter | solution.py:253
  338.6 80.4 %reduce-scatter.26.cloned.1.call-start = ((), (), s32[]{:S(2)}) async-start(), calls=%async_computation.26 | async-start | bytes 4718592 | tf_op jit(solution)/shard_map/reduce_scatter | solution.py:256
  357.4 7.0 copy-start.26
  364.4 54.6 %copy-start.20 = (bf16[384,768]{1,0:T(8,128)(2,1)S(1)}, bf16[384,768]{1,0:T(8,128)(2,1)}, u32[]{:S(2)}) copy-start(bf16[384,768]{1,0:T(8,128)(2,1)} %reduce-scatter.14.cloned.1.call-done) | copy-start | bytes 1769476
  364.4 54.6 %copy-start.21 = (bf16[384,768]{1,0:T(8,128)(2,1)S(1)}, bf16[384,768]{1,0:T(8,128)(2,1)}, u32[]{:S(2)}) copy-start(bf16[384,768]{1,0:T(8,128)(2,1)} %reduce-scatter.20.cloned.1.call-done) | copy-start | bytes 1769476
  (25 other events, 48.1 us)
Sparse Core Ops, SparseCore 0:
  9.6 11.9 all-gather.17
  23.1 10.3 all-gather.11
  35.1 10.3 all-gather.15
  47.5 28.3 all-gather.19
  77.8 27.1 all-gather.13
  106.5 9.2 all-gather.21
  117.3 13.2 all-gather.23
  132.2 13.2 all-gather.25
  147.0 13.2 all-gather.27
  269.4 27.2 reduce-scatter.9
  299.0 26.0 reduce-scatter.11
  327.8 8.6 reduce-scatter.13
  339.4 9.8 reduce-scatter.19
  352.0 9.8 reduce-scatter.15
  364.7 9.8 reduce-scatter.17
  377.3 12.0 reduce-scatter.21
  392.1 12.0 reduce-scatter.23
  406.9 12.0 reduce-scatter.25
where the time goes:
time: 1020 us; the launch traced here: 1010 us
  blocking collectives  593 us (58%)
  waiting for transfers between devices  178 us (17%)
  matrix products  174 us (17%)
  local copies, waits for them, and re-layouts  28.9 us (3%)
  other arithmetic  21.5 us (2%)
  between operations  16.3 us (2%)
    psum x1, blocking collectives, on_device(): lax.psum((shards[0], shards[1], shards[2], shards[3], shards[4], shards[5...  586 us
    dot_general x3, matrix products, piece_scores(): jnp.einsum('qhd,khd->hqk', query_heads, key_heads, preferred_element_type...  29.3 us
    all_gather x1, waiting for transfers between devices, on_device(): key_piece = lax.all_gather(key_rows, 'ctx', axis=0, tiled=True)  27.1 us
    reduce_scatter x1, waiting for transfers between devices, on_device(): lax.psum_scatter(value_terms.reshape(whole_rows, D).astype(jnp.bfloat16),...  25.3 us
    reduce_scatter x1, waiting for transfers between devices, on_device(): lax.psum_scatter(key_terms.reshape(whole_rows, D).astype(jnp.bfloat16), '...  21.3 us
  transfers between devices with their start and end apart: 18, of which 14 were waited for; matrix products, arithmetic and copies ran while one was open for 11% of the time, Pallas kernels for 0%

commit v1 on v0

v1 whole, which is shorter than its diff:
```python
import functools

import jax
import jax.numpy as jnp
from jax import lax
from jax.experimental import pallas as pl
from jax.experimental.pallas import tpu as pltpu
from jax.sharding import PartitionSpec as P

D = 768
HEAD_DIM = 64
PAIR = 2 * HEAD_DIM
EPSILON = 1e-06
DEAD = -1e30
VMEM = 60 << 20

F32 = jnp.float32
BF = jnp.bfloat16
NN = (((1,), (0,)), ((), ()))
NT = (((1,), (1,)), ((), ()))
SMEM = pl.BlockSpec(memory_space=pltpu.SMEM)


def mm(left, right, dims):
    return lax.dot_general(left, right, dims, preferred_element_type=F32)


def whole(shape):
    return pl.BlockSpec(shape, lambda j: (0,) * len(shape))


def call(kernel, grid, in_specs, out_specs, out_shape, flops, moved, name, scratch=()):
    return pl.pallas_call(
        kernel,
        grid=grid,
        in_specs=in_specs,
        out_specs=out_specs,
        out_shape=out_shape,
        scratch_shapes=list(scratch),
        compiler_params=pltpu.CompilerParams(vmem_limit_bytes=VMEM),
        cost_estimate=pl.CostEstimate(flops=flops, bytes_accessed=moved, transcendentals=0),
        name=name,
    )


def shape(dims, dtype):
    return jax.ShapeDtypeStruct(dims, dtype)


def rms_scale(values):
    return lax.rsqrt(jnp.mean(values * values, axis=-1, keepdims=True) + EPSILON)


def stack(core, own, other):
    return jnp.concatenate(
        [jnp.where(core == 0, own, other), jnp.where(core == 0, other, own)], axis=0
    )


def gain_row(core, own, other, index):
    own = own[index : index + 1, :].astype(F32)
    other = other[index : index + 1, :].astype(F32)
    return jnp.concatenate(
        [jnp.where(core == 0, own, other), jnp.where(core == 0, other, own)], axis=1
    )


def put_halves(core, value, own_ref, other_ref):
    half = value.shape[0] // 2
    low, high = value[:half], value[half:]
    own_ref[...] = jnp.where(core == 0, low, high).astype(own_ref.dtype)
    other_ref[...] = jnp.where(core == 0, high, low).astype(other_ref.dtype)


def project_kernel(count, core_ref, x_ref, gain_own, gain_other, *refs):
    core = core_ref[0]
    weights, outs, normed_ref = refs[: 2 * count], refs[2 * count :], refs[2 * count]

    @pl.when(pl.program_id(0) == 0)
    def _():
        x = x_ref[...].astype(F32)
        gain = gain_row(core, gain_own[...], gain_other[...], 0)
        normed_ref[...] = (x * rms_scale(x) * gain).astype(BF)

    normed = normed_ref[...]
    for i in range(count):
        weight = stack(core, weights[2 * i][...], weights[2 * i + 1][...])
        outs[1 + i][...] = mm(normed, weight, NN).astype(BF)


def project(core, x, gains, weights):
    rows, count, cols = x.shape[0], len(weights), 256
    weight_spec = pl.BlockSpec((D // 2, cols), lambda j: (0, j))
    out_spec = pl.BlockSpec((rows, cols), lambda j: (0, j))
    return call(
        functools.partial(project_kernel, count),
        (D // cols,),
        [SMEM, whole((rows, D))] + [whole((2, D // 2))] * 2 + [weight_spec] * (2 * count),
        [whole((rows, D))] + [out_spec] * count,
        [shape((rows, D), BF)] * (1 + count),
        2 * rows * D * D * count,
        2 * D * (rows * (2 + count) + D * count),
        "project",
    )(core, x, *gains, *(part for pair in weights for part in pair))


def split3(value):
    high = value.astype(BF).astype(F32)
    rest = value - high
    mid = rest.astype(BF).astype(F32)
    return high, mid, rest - mid


def key_extra(limits_ref, rows, blocks):
    lane = lax.broadcasted_iota(jnp.int32, (rows, PAIR), 1) % HEAD_DIM
    row = lax.broadcasted_iota(jnp.int32, (rows, PAIR), 0)
    pieces = []
    for block in range(blocks):
        bias = jnp.where(row < limits_ref[block], 0.0, DEAD)
        pieces.append(
            jnp.where(lane < 3, 1.0, jnp.where(lane == 3, bias, 0.0)).astype(BF)
        )
    return jnp.concatenate(pieces, axis=0) if blocks > 1 else pieces[0]


def joined(refs):
    return jnp.concatenate([ref[...] for ref in refs], axis=0) if len(refs) > 1 else refs[0][...]


def place3(lane, base, parts, into):
    for i in (2, 1, 0):
        into = jnp.where(lane == base + i, parts[i], into)
    return into


def attend_kernel(blocks, limits_ref, q_ref, *refs):
    keys, values = joined(refs[:blocks]), joined(refs[blocks : 2 * blocks])
    wide_ref, low_ref, extra_ref = refs[2 * blocks :]
    rows, total = q_ref.shape[0], keys.shape[0]
    queries = q_ref[...] * jnp.asarray(HEAD_DIM**-0.5, BF)
    extra = key_extra(limits_ref, rows, blocks)
    lane = lax.broadcasted_iota(jnp.int32, (rows, PAIR), 1)
    key_lane = lax.broadcasted_iota(jnp.int32, (total, PAIR), 1)
    log_lanes = jnp.where(lane % HEAD_DIM == 3, 1.0, 0.0)
    bias_lane = log_lanes.astype(BF)
    heads = []
    for head in range(2):
        mine = lane // HEAD_DIM == head
        key_mine = key_lane // HEAD_DIM == head
        scores = mm(
            jnp.where(mine, queries, bias_lane), jnp.where(key_mine, keys, extra), NT
        )
        top = jnp.max(scores, axis=-1, keepdims=True)
        weights = jnp.exp(scores - top)
        sums = jnp.sum(weights, axis=-1, keepdims=True)
        heads.append(mm(weights.astype(BF), values, NN) / sums)
        log_lanes = place3(
            lane, HEAD_DIM * (1 - head), split3(-(top + jnp.log(sums))), log_lanes
        )
    attended = jnp.where(lane < HEAD_DIM, heads[0], heads[1])
    wide_ref[...] = attended
    low_ref[...] = attended.astype(BF)
    extra_ref[...] = log_lanes.astype(BF)


def attend(limits, queries, keys, values):
    rows, blocks = queries.shape[0], len(keys)
    spec = pl.BlockSpec((rows, PAIR), lambda j: (0, j))
    return call(
        functools.partial(attend_kernel, blocks),
        (D // PAIR,),
        [SMEM] + [spec] * (1 + 2 * blocks),
        [spec] * 3,
        [shape((rows, D), F32), shape((rows, D), BF), shape((rows, D), BF)],
        16 * rows * rows * blocks * D,
        2 * rows * D * (5 + 2 * blocks),
        "attend",
    )(limits, queries, *keys, *values)


def attend_back_kernel(blocks, core_ref, limits_ref, q_ref, *refs):
    keys, values = joined(refs[:blocks]), joined(refs[blocks : 2 * blocks])
    dmb_ref, wide_ref, low_ref, extra_ref, wo_own, wo_other = refs[2 * blocks : 2 * blocks + 6]
    outs = refs[2 * blocks + 6 :]
    dq_ref, dk_refs, dv_refs = outs[0], outs[1 : 1 + blocks], outs[1 + blocks : 1 + 2 * blocks]
    out_own, out_other = outs[1 + 2 * blocks :]
    step = pl.program_id(0)
    count = pl.num_programs(0) // 2
    rows, total = q_ref.shape[0], keys.shape[0]
    scale = jnp.asarray(HEAD_DIM**-0.5, BF)
    queries = q_ref[...] * scale
    dmb = dmb_ref[...]
    weight = jnp.where(step < count, wo_other[...], wo_own[...])
    grads = mm(dmb, weight, NT).astype(BF)
    out_term = mm(low_ref[...].T, dmb, NN).astype(BF)

    @pl.when(step < count)
    def _():
        out_other[...] = out_term

    @pl.when(step >= count)
    def _():
        out_own[...] = out_term

    log_lanes = extra_ref[...]
    extra = key_extra(limits_ref, rows, blocks)
    lane = lax.broadcasted_iota(jnp.int32, (rows, PAIR), 1)
    key_lane = lax.broadcasted_iota(jnp.int32, (total, PAIR), 1)
    product = grads.astype(F32) * wide_ref[...]
    delta_lanes = jnp.zeros((rows, PAIR), F32)
    for head in range(2):
        mine = lane // HEAD_DIM == head
        delta = -jnp.sum(jnp.where(mine, product, 0.0), axis=-1, keepdims=True)
        delta_lanes = place3(lane, HEAD_DIM * (1 - head), split3(delta), delta_lanes)
    delta_lanes = delta_lanes.astype(BF)
    keys_turned = (keys * scale).T
    none = jnp.zeros((rows, PAIR), BF)
    dk = dv = 0.0
    dqs = []
    for head in range(2):
        mine = lane // HEAD_DIM == head
        key_mine = key_lane // HEAD_DIM == head
        probs = jnp.exp(
            mm(jnp.where(key_mine, keys, extra), jnp.where(mine, queries, log_lanes), NT)
        )
        shifted = mm(
            jnp.where(key_mine, values, extra), jnp.where(mine, grads, delta_lanes), NT
        )
        dscores = (probs * shifted).astype(BF)
        dv = dv + mm(probs.astype(BF), jnp.where(mine, grads, none), NN)
        dk = dk + mm(dscores, jnp.where(mine, queries, none), NN)
        dqs.append(mm(keys_turned[head * HEAD_DIM : (head + 1) * HEAD_DIM], dscores, NN))
    dq_ref[...] = jnp.concatenate(dqs, axis=0).T.astype(BF)
    for block in range(blocks):
        dk_refs[block][...] = dk[block * rows : (block + 1) * rows].astype(BF)
        dv_refs[block][...] = dv[block * rows : (block + 1) * rows].astype(BF)


def attend_back(core, limits, queries, keys, values, dmb, wide, low, extra, out_weight):
    rows, blocks = queries.shape[0], len(keys)
    pairs = D // PAIR
    half = pairs // 2

    def at(j, core_ref):
        return (j + half * (1 - core_ref[0])) % pairs

    spec = pl.BlockSpec((rows, PAIR), lambda j, core_ref, limits_ref: (0, at(j, core_ref)))
    full = pl.BlockSpec((rows, D), lambda j, core_ref, limits_ref: (0, 0))
    other_spec = pl.BlockSpec(
        (PAIR, D), lambda j, core_ref, limits_ref: (jnp.minimum(j, half - 1), 0)
    )
    own_spec = pl.BlockSpec(
        (PAIR, D), lambda j, core_ref, limits_ref: (jnp.maximum(j - half, 0), 0)
    )
    results = pl.pallas_call(
        functools.partial(attend_back_kernel, blocks),
        grid_spec=pltpu.PrefetchScalarGridSpec(
            num_scalar_prefetch=2,
            grid=(pairs,),
            in_specs=[spec] * (1 + 2 * blocks) + [full, spec, spec, spec, own_spec, other_spec],
            out_specs=[spec] * (1 + 2 * blocks) + [own_spec, other_spec],
        ),
        out_shape=[shape((rows, D), BF)] * (1 + 2 * blocks) + [shape((D // 2, D), BF)] * 2,
        compiler_params=pltpu.CompilerParams(vmem_limit_bytes=VMEM),
        cost_estimate=pl.CostEstimate(
            flops=40 * rows * rows * blocks * D,
            bytes_accessed=2 * rows * D * (8 + 4 * blocks),
            transcendentals=0,
        ),
        name="attend_back",
    )(core, limits, queries, *keys, *values, dmb, wide, low, extra, *out_weight)
    return results[0], results[1 : 1 + blocks], results[1 + blocks : 1 + 2 * blocks], results[1 + 2 * blocks :]


CURVE = 0.7978845608028654
CUBIC = 0.044715


def ffn_part(core, step, h2, h2_turned, dyb, weights, grads, acc_out, acc_back):
    gate_own, gate_other, up_own, up_other, down_own, down_other = weights
    dgate_own, dgate_other, dup_own, dup_other, ddown_own, ddown_other = grads
    gate_weight = stack(core, gate_own[...], gate_other[...])
    up_weight = stack(core, up_own[...], up_other[...])
    down_weight = jnp.where(step == core, down_own[...], down_other[...])
    gate = mm(h2, gate_weight, NN)
    up = mm(h2, up_weight, NN)
    dn = mm(dyb, down_weight, NT)
    square = gate * gate
    bent = jnp.tanh(CURVE * gate * (1.0 + CUBIC * square))
    rise = 0.5 * (1.0 + bent)
    bulge = gate * rise
    slope = rise + 0.5 * gate * (1.0 - bent * bent) * (CURVE * (1.0 + 3.0 * CUBIC * square))
    hidden = (bulge * up).astype(BF)
    dgate = (dn * up * slope).astype(BF)
    dup = (dn * bulge).astype(BF)
    ddown = mm(hidden.T, dyb, NN).astype(BF)

    @pl.when(step == core)
    def _():
        ddown_own[...] = ddown

    @pl.when(step != core)
    def _():
        ddown_other[...] = ddown

    put_halves(core, mm(h2_turned, dgate, NN), dgate_own, dgate_other)
    put_halves(core, mm(h2_turned, dup, NN), dup_own, dup_other)
    acc_out[...] += mm(hidden, down_weight, NN)
    acc_back[...] += mm(dgate, gate_weight, NT) + mm(dup, up_weight, NT)


def live_grad(limits_ref, grad_ref):
    rows = grad_ref.shape[0]
    live = lax.broadcasted_iota(jnp.int32, (rows, D), 0) < limits_ref[0]
    return jnp.where(live, grad_ref[...].astype(F32), 0.0)


def ffn_first_kernel(core_ref, limits_ref, x_ref, a_ref, wo_own, wo_other, gain_own, gain_other, grad_ref, *refs):
    core, step = core_ref[0], pl.program_id(0)
    weights, outs = refs[:6], refs[6:]
    m_ref, h2_ref, acc_out, acc_back = outs[:4]
    grads, (turned,) = outs[4:10], outs[10:]

    @pl.when(step == 0)
    def _():
        weight = stack(core, wo_own[...], wo_other[...])
        m = x_ref[...].astype(F32) + mm(a_ref[...], weight, NN)
        gain = gain_row(core, gain_own[...], gain_other[...], 1)
        m_ref[...] = m
        h2 = (m * rms_scale(m) * gain).astype(BF)
        h2_ref[...] = h2
        turned[...] = h2.T
        acc_out[...] = jnp.zeros_like(acc_out)
        acc_back[...] = jnp.zeros_like(acc_back)

    dyb = live_grad(limits_ref, grad_ref).astype(BF)
    ffn_part(core, step, h2_ref[...], turned[...], dyb, weights, grads, acc_out, acc_back)


def ffn_last_kernel(core_ref, limits_ref, m_ref, h2_ref, gain_own, gain_other, grad_ref, out_in, back_in, *refs):
    core, step = core_ref[0], pl.program_id(0)
    weights, outs = refs[:6], refs[6:]
    output_ref, dm_ref, dmb_ref, dgain_ref = outs[:4]
    grads, (turned, acc_out, acc_back) = outs[4:10], outs[10:]

    @pl.when(step == 0)
    def _():
        turned[...] = h2_ref[...].T
        acc_out[...] = out_in[...]
        acc_back[...] = back_in[...]

    dy = live_grad(limits_ref, grad_ref)
    ffn_part(core, step, h2_ref[...], turned[...], dy.astype(BF), weights, grads, acc_out, acc_back)

    @pl.when(step == pl.num_programs(0) - 1)
    def _():
        m = m_ref[...]
        output_ref[...] = (m + acc_out[...]).astype(BF)
        gain = gain_row(core, gain_own[...], gain_other[...], 1)
        scale = rms_scale(m)
        back = acc_back[...]
        dgain_ref[...] = jnp.sum(back * m * scale, axis=0, keepdims=True)
        scaled = back * gain
        dm = dy + scale * scaled - m * (scale * scale * scale) * jnp.mean(
            scaled * m, axis=-1, keepdims=True
        )
        dm_ref[...] = dm
        dmb_ref[...] = dm.astype(BF)


def ffn_specs(part, hidden):
    wide = hidden // 4
    gate_spec = pl.BlockSpec((D // 2, wide), lambda j: (0, part + 2 * j))
    down_spec = pl.BlockSpec((wide, D), lambda j: (part, 0))
    grad_spec = pl.BlockSpec((D // 2, wide), lambda j: (0, j))
    weight_specs = [gate_spec] * 4 + [down_spec] * 2
    grad_specs = [grad_spec] * 4 + [whole((wide, D))] * 2
    grad_shapes = [shape((D // 2, 2 * wide), BF)] * 4 + [shape((wide, D), BF)] * 2
    return weight_specs, grad_specs, grad_shapes


def ffn_first(core, limits, x, attended, out_weight, gains, grad, weights):
    rows, hidden = x.shape[0], weights[0].shape[1]
    weight_specs, grad_specs, grad_shapes = ffn_specs(0, hidden)
    row = whole((rows, D))
    return call(
        ffn_first_kernel,
        (2,),
        [SMEM, SMEM, row, row] + [whole((D // 2, D))] * 2 + [whole((2, D // 2))] * 2 + [row] + weight_specs,
        [row] * 4 + grad_specs,
        [shape((rows, D), F32), shape((rows, D), BF), shape((rows, D), F32), shape((rows, D), F32)] + grad_shapes,
        9 * rows * D * hidden,
        2 * D * (rows * 10 + hidden * 3),
        "ffn_first",
        [pltpu.VMEM((D, rows), BF)],
    )(core, limits, x, attended, *out_weight, *gains, grad, *weights)


def ffn_last(core, limits, m, h2, gains, grad, acc_out, acc_back, weights):
    rows, hidden = h2.shape[0], weights[0].shape[1]
    weight_specs, grad_specs, grad_shapes = ffn_specs(1, hidden)
    row = whole((rows, D))
    return call(
        ffn_last_kernel,
        (2,),
        [SMEM, SMEM, row, row] + [whole((2, D // 2))] * 2 + [row] * 3 + weight_specs,
        [row] * 3 + [whole((1, D))] + grad_specs,
        [shape((rows, D), BF), shape((rows, D), F32), shape((rows, D), BF), shape((1, D), F32)] + grad_shapes,
        9 * rows * D * hidden,
        2 * D * (rows * 10 + hidden * 3),
        "ffn_last",
        [pltpu.VMEM((D, rows), BF), pltpu.VMEM((rows, D), F32), pltpu.VMEM((rows, D), F32)],
    )(core, limits, m, h2, *gains, grad, acc_out, acc_back, *weights)


def project_grads_kernel(blocks, core_ref, dq_ref, *refs):
    core = core_ref[0]
    dks, dvs, normed = refs[:blocks], refs[blocks : 2 * blocks], refs[2 * blocks : 3 * blocks]
    outs, turned = refs[3 * blocks : 3 * blocks + 6], refs[3 * blocks + 6]

    @pl.when(pl.program_id(0) == 0)
    def _():
        for block in range(blocks):
            rows = normed[block].shape[0]
            turned[:, block * rows : (block + 1) * rows] = normed[block][...].T

    rows = dq_ref.shape[0]
    put_halves(core, mm(turned[:, :rows], dq_ref[...], NN), outs[0], outs[1])
    put_halves(core, mm(turned[...], joined(dks), NN), outs[2], outs[3])
    put_halves(core, mm(turned[...], joined(dvs), NN), outs[4], outs[5])


def project_grads(core, dq, dks, dvs, normed):
    rows, blocks, cols = dq.shape[0], len(dks), 256
    spec = pl.BlockSpec((rows, cols), lambda j: (0, j))
    out_spec = pl.BlockSpec((D // 2, cols), lambda j: (0, j))
    return call(
        functools.partial(project_grads_kernel, blocks),
        (D // cols,),
        [SMEM] + [spec] * (1 + 2 * blocks) + [whole((rows, D))] * blocks,
        [out_spec] * 6,
        [shape((D // 2, D), BF)] * 6,
        2 * rows * D * D * (1 + 2 * blocks),
        2 * D * (rows * (1 + 3 * blocks) + D * 3),
        "project_grads",
        [pltpu.VMEM((D, rows * blocks), BF)],
    )(core, dq, *dks, *dvs, *normed)


def project_back_kernel(blocks, core_ref, gain_own, gain_other, dq_ref, *refs):
    core, block = core_ref[0], pl.program_id(0)
    dks, dvs, xs = refs[:blocks], refs[blocks : 2 * blocks], refs[2 * blocks : 3 * blocks]
    weights = refs[3 * blocks : 3 * blocks + 6]
    outs, dgain_ref = refs[3 * blocks + 6 : 4 * blocks + 6], refs[4 * blocks + 6]
    query = stack(core, weights[0][...], weights[1][...])
    key = stack(core, weights[2][...], weights[3][...])
    value = stack(core, weights[4][...], weights[5][...])
    total = jnp.zeros((1, D), F32)
    for block in range(blocks):
        back = mm(dks[block][...], key, NT) + mm(dvs[block][...], value, NT)
        if block == 0:
            back = back + mm(dq_ref[...], query, NT)
        x = xs[block][...].astype(F32)
        total = total + jnp.sum(back * x * rms_scale(x), axis=0, keepdims=True)
        outs[block][...] = back.astype(outs[block].dtype)
    dgain_ref[...] = total


def project_back(core, gains, dq, dks, dvs, xs, weights):
    rows, blocks = dq.shape[0], len(dks)
    row = whole((rows, D))
    return call(
        functools.partial(project_back_kernel, blocks),
        (1,),
        [SMEM] + [whole((2, D // 2))] * 2 + [row] * (1 + 3 * blocks) + [whole((D // 2, D))] * 6,
        [row] * blocks + [whole((1, D))],
        [shape((rows, D), F32)] + [shape((rows, D), BF)] * (blocks - 1) + [shape((1, D), F32)],
        2 * rows * D * D * (1 + 2 * blocks),
        2 * D * (rows * (1 + 4 * blocks) + D * 3),
        "project_back",
    )(core, *gains, dq, *dks, *dvs, *xs, *(part for pair in weights for part in pair))


def input_grad_kernel(core_ref, gain_own, gain_other, x_ref, dm_ref, own_ref, *refs):
    x = x_ref[...].astype(F32)
    scale = rms_scale(x)
    back = own_ref[...]
    for ref in refs[:-1]:
        back = back + ref[...].astype(F32)
    scaled = back * gain_row(core_ref[0], gain_own[...], gain_other[...], 0)
    refs[-1][...] = (
        dm_ref[...]
        + scale * scaled
        - x * (scale * scale * scale) * jnp.mean(scaled * x, axis=-1, keepdims=True)
    ).astype(BF)


def input_grad_of(core, gains, x, dm, own, received):
    rows, cut = x.shape[0], 4
    spec = pl.BlockSpec((rows // cut, D), lambda j: (j, 0))
    return call(
        input_grad_kernel,
        (cut,),
        [SMEM] + [whole((2, D // 2))] * 2 + [spec] * (3 + len(received)),
        spec,
        shape((rows, D), BF),
        rows * D,
        2 * D * rows * 8,
        "input_grad",
    )(core, *gains, x, dm, own, *received)


def swap(value, axis, mask):
    count = lax.axis_size(axis)
    return lax.ppermute(value, axis, [(i, i ^ mask) for i in range(count)])


def bits_of(axis):
    index, out, mask = lax.axis_index(axis), [], 1
    while mask < lax.axis_size(axis):
        out.append(((index // mask) % 2, axis, mask))
        mask *= 2
    return out


def add(left, right):
    return (left.astype(F32) + right.astype(F32)).astype(BF)


def sum_over_chips(arrays):
    ctx, grp = bits_of("ctx"), bits_of("grp")
    cube = [ctx[0], grp[0], grp[1]]
    rest = grp[2:] + ctx[1:]
    orders = [[cube[(i + s) % 3] for i in range(3)] for s in range(len(arrays))]
    current = list(arrays)
    for stage in range(3):
        kept, sent = [], []
        for value, order in zip(current, orders):
            bit, axis, mask = order[stage]
            half = value.shape[0] // 2
            kept.append(lax.dynamic_slice_in_dim(value, bit * half, half, 0))
            sent.append(swap(lax.dynamic_slice_in_dim(value, (1 - bit) * half, half, 0), axis, mask))
        current = [add(k, s) for k, s in zip(kept, sent)]
    for _, axis, mask in rest:
        current = [add(c, swap(c, axis, mask)) for c in current]
    for stage in (2, 1, 0):
        received = [swap(v, o[stage][1], o[stage][2]) for v, o in zip(current, orders)]
        current = [
            jnp.concatenate(
                [jnp.where(o[stage][0] == 0, v, r), jnp.where(o[stage][0] == 0, r, v)], axis=0
            )
            for v, r, o in zip(current, received, orders)
        ]
    return current


def on_device(
    tokens,
    lengths,
    query_weight,
    key_weight,
    value_weight,
    output_weight,
    gate_weight,
    up_weight,
    down_weight,
    attn_gain,
    ffn_gain,
    out_grad,
):
    blocks = lax.axis_size("ctx")
    x, grad = tokens[0], out_grad[0]
    rows = x.shape[0]
    place = lax.axis_index("ctx")
    core = lax.axis_index("wsh").astype(jnp.int32)[None]
    limits = jnp.clip(
        lengths[0] - rows * jnp.stack([place ^ r for r in range(blocks)]).astype(jnp.int32), 0, rows
    )

    def both(own):
        return (own, swap(own, "wsh", 1))

    gains = both(jnp.stack([attn_gain, ffn_gain]))
    xs = [x] + [swap(x, "ctx", r) for r in range(1, blocks)]
    wq, wk, wv, wo = both(query_weight), both(key_weight), both(value_weight), both(output_weight)
    wg, wu, wd = both(gate_weight), both(up_weight), both(down_weight)

    h1, queries, key, value = project(core, x, gains, [wq, wk, wv])
    normed, keys, values = [h1], [key], [value]
    for peer in xs[1:]:
        h1, key, value = project(core, peer, gains, [wk, wv])
        normed.append(h1)
        keys.append(key)
        values.append(value)
    wide, low, extra = attend(limits, queries, keys, values)
    ffn_weights = (*wg, *wu, *wd)
    m, h2, acc_out, acc_back, *grads = ffn_first(
        core, limits, x, low, wo, gains, grad, ffn_weights
    )

    def over_cores(pairs):
        return [add(own, swap(other, "wsh", 1)) for own, other in pairs]

    def pairs_of(values):
        return list(zip(values[0::2], values[1::2]))

    first = sum_over_chips(over_cores(pairs_of(grads)))
    output, dm, dmb, dgain_ffn, *grads = ffn_last(
        core, limits, m, h2, gains, grad, acc_out, acc_back, ffn_weights
    )
    second = sum_over_chips(over_cores(pairs_of(grads)))
    dq, dks, dvs, out_terms = attend_back(
        core, limits, queries, keys, values, dmb, wide, low, extra, wo
    )
    grads = project_grads(core, dq, dks, dvs, normed)
    third = sum_over_chips(over_cores(pairs_of(grads) + [tuple(out_terms)]))
    *backs, dgain_attn = project_back(core, gains, dq, dks, dvs, xs, [wq, wk, wv])
    received = [swap(back, "ctx", r) for r, back in enumerate(backs) if r]
    input_grad = input_grad_of(core, gains, x, dm, backs[0], received)
    dgains = lax.psum(jnp.concatenate([dgain_attn, dgain_ffn], axis=0), ("grp", "ctx", "wsh"))
    dgains = lax.dynamic_slice_in_dim(dgains, core[0] * (D // 2), D // 2, 1)

    def spread(early, late):
        cut = early.shape[1] // 2
        return jnp.concatenate(
            [early[:, :cut], late[:, :cut], early[:, cut:], late[:, cut:]], axis=1
        ).astype(F32)

    return (
        output[None],
        input_grad[None],
        third[0].astype(F32),
        third[1].astype(F32),
        third[2].astype(F32),
        third[3].astype(F32),
        spread(first[0], second[0]),
        spread(first[1], second[1]),
        jnp.concatenate([first[2], second[2]], axis=0).astype(F32),
        dgains[0],
        dgains[1],
    )


def solution(mesh):
    rows, weights, vector = P(("grp", "wsh"), "ctx", None), P("wsh", None), P("wsh")
    in_specs = (rows, P(("grp", "wsh"))) + (weights,) * 7 + (vector,) * 2 + (rows,)
    out_specs = (rows,) * 2 + (weights,) * 7 + (vector,) * 2
    return jax.shard_map(
        on_device, mesh=mesh, in_specs=in_specs, out_specs=out_specs, check_vma=False
    )
```

time: 1020 us -> 442 us (0.43)
  blocking collectives: 593 us -> 40.9 us
  matrix products: 174 us -> 0 us
  Pallas kernels: 0 us -> 107 us
  starting transfers between devices: 0.89 us -> 80 us
  local copies, waits for them, and re-layouts: 28.9 us -> 11.2 us
  waiting for transfers between devices: 178 us -> 163 us
  between operations: 16.3 us -> 3.39 us
    psum x1, blocking collectives: 586 us -> 40.9 us  [on_device(): lax.psum(jnp.concatenate([dgain_attn, dgain_ffn], axis=0), ('grp', 'ctx',...]
    dot_general x33 -> x0, matrix products: 174 us -> none  [the longest x3 29.3 us: piece_scores(): jnp.einsum('qhd,khd->hqk', query_heads, key_heads, preferred_element_type...]
    ppermute x0 -> x90, waiting for transfers between devices: none -> 163 us  [swap(): return lax.ppermute(value, axis, [(i, i ^ mask) for i in range(count)])]
    pallas_call x0 -> x9, Pallas kernels: none -> 107 us  [the longest x1 26.8 us: attend_back(): pl.pallas_call(functools.partial(attend_back_kernel, blocks), grid_spec=p...]
    reduce_scatter x9 -> x0, waiting for transfers between devices: 98.4 us -> none  [the longest x1 25.3 us: on_device(): lax.psum_scatter(value_terms.reshape(whole_rows, D).astype(jnp.bfloat16),...]
    ppermute x0 -> x90, starting transfers between devices: none -> 80 us  [swap(): return lax.ppermute(value, axis, [(i, i ^ mask) for i in range(count)])]
    all_gather x9 -> x0, waiting for transfers between devices: 73.8 us -> none  [the longest x1 27.1 us: on_device(): key_piece = lax.all_gather(key_rows, 'ctx', axis=0, tiled=True)]
    convert_element_type x6 -> x57, other arithmetic: 1.09 us -> 24.3 us  [the longest x50 11.3 us: add(): return (left.astype(F32) + right.astype(F32)).astype(BF)]
  transfers between devices with their start and end apart: 18 -> 90, of which waited for: 14 -> 38; matrix products, arithmetic and copies ran while one was open for 11% -> 8% of each run, Pallas kernels for 0% -> 21%
where the time goes in v1:
time: 442 us; the launch traced here: 433 us
  waiting for transfers between devices  163 us (37%)
  Pallas kernels  107 us (24%)
  starting transfers between devices  80 us (18%)
  blocking collectives  40.9 us (9%)
  other arithmetic  28.4 us (6%)
  local copies, waits for them, and re-layouts  11.2 us (3%)
    ppermute x90, waiting for transfers between devices, swap(): return lax.ppermute(value, axis, [(i, i ^ mask) for i in range(count)])  163 us
    ppermute x90, starting transfers between devices, swap(): return lax.ppermute(value, axis, [(i, i ^ mask) for i in range(count)])  80 us
    psum x1, blocking collectives, on_device(): lax.psum(jnp.concatenate([dgain_attn, dgain_ffn], axis=0), ('grp', 'ctx',...  40.9 us
    pallas_call x1, Pallas kernels, attend_back(): pl.pallas_call(functools.partial(attend_back_kernel, blocks), grid_spec=p...  26.8 us
    pallas_call x1, Pallas kernels, ffn_last(): call(ffn_last_kernel, (2,), [SMEM, SMEM, row, row] + [whole((2, D // 2))]...  17.3 us
    pallas_call x1, Pallas kernels, attend(): call(functools.partial(attend_kernel, blocks), (D // PAIR,), [SMEM] + [sp...  15.4 us
    pallas_call x1, Pallas kernels, ffn_first(): call(ffn_first_kernel, (2,), [SMEM, SMEM, row, row] + [whole((D // 2, D))...  15.2 us
    pallas_call x2, Pallas kernels, project(): call(functools.partial(project_kernel, count), (D // cols,), [SMEM, whole...  11.5 us
  transfers between devices with their start and end apart: 90, of which 38 were waited for; matrix products, arithmetic and copies ran while one was open for 8% of the time, Pallas kernels for 21%

profile of v1, /device:TPU:0, one launch (start us, length us, event | category | flops | bytes accessed | tf_op | source)
XLA Modules:
  0.0 433.4 jit_solution(434858441131497460)
XLA Ops:
  8.5 3.7 collective-permute-done.1.refs_1_.refs_7_
  12.4 6.1 %project.2 = (bf16[512,768]{1,0:T(8,128)(2,1)}, bf16[512,768]{1,0:T(8,128)(2,1)}, bf16[512,768]{1,0:T(8,128)(2,1)}, bf16[512,768]{1,0:T(8,128)(2,1)}) custom-call(s32[1]{0:T(128)} %bitcast.core_ref, bf16[512,768]{1,0:T(8,128)(2,1)} %bitcast.10, bf16[2,384]{1,0:T(2,128)(2,1)} %copy-done.22, bf16[2,384]{1,0:T(2,128)(2,1)} %copy-done.24, ...), custom_call_target="tpu_custom_call" | custom-call | flops 1811939328 | bytes 7471104 | tf_op jit(solution)/shard_map/project/pallas_call | solution.py:95
  18.5 6.7 %collective-permute-done.4.x_ref.refs_5_ = bf16[512,768]{1,0:T(8,128)(2,1)S(1)} collective-permute-done((bf16[512,768]{1,0:T(8,128)(2,1)}, bf16[512,768]{1,0:T(8,128)(2,1)S(1)}, u32[]{:S(2)}, u32[]{:S(2)}) %collective-permute-start.4) | collective-permute-done | bytes 786464 | tf_op jit(solution)/shard_map/ppermute | solution.py:515
  26.1 5.4 %project.3 = (bf16[512,768]{1,0:T(8,128)(2,1)}, bf16[512,768]{1,0:T(8,128)(2,1)}, bf16[512,768]{1,0:T(8,128)(2,1)}) custom-call(s32[1]{0:T(128)} %bitcast.core_ref, bf16[512,768]{1,0:T(8,128)(2,1)} %copy-done.26, bf16[2,384]{1,0:T(2,128)(2,1)} %copy-done.22, bf16[2,384]{1,0:T(2,128)(2,1)} %copy-done.24, bf16[384,768]{1,0:T(8,128)(2,1)} %refs_8_.3, ...), custom_call_target="tpu_custom_call" | custom-call | flops 1207959552 | bytes 5505024 | tf_op jit(solution)/shard_map/project/pallas_call | solution.py:95
  31.4 15.4 %attend.1 = (f32[512,768]{1,0:T(8,128)}, bf16[512,768]{1,0:T(8,128)(2,1)}, bf16[512,768]{1,0:T(8,128)(2,1)}) custom-call(s32[2]{0:T(128)} %fusion.22.limits_ref, bf16[512,768]{1,0:T(8,128)(2,1)} %get-tuple-element.57.q_ref, bf16[512,768]{1,0:T(8,128)(2,1)} %get-tuple-element.58.refs_0_, bf16[512,768]{1,0:T(8,128)(2,1)} %get-tuple-element.59.refs_1_, ...), custom_call_target="tpu_custom_call" | custom-call | flops 6442450944 | bytes 7077888 | tf_op jit(solution)/shard_map/attend/pallas_call | solution.py:169
  48.0 15.2 %ffn_first.1 = (f32[512,768]{1,0:T(8,128)}, bf16[512,768]{1,0:T(8,128)(2,1)}, f32[512,768]{1,0:T(8,128)}, f32[512,768]{1,0:T(8,128)}, bf16[384,1024]{1,0:T(8,128...) custom-call(s32[1]{0:T(128)} %bitcast.core_ref, ...), custom_call_target="tpu_custom_call" | custom-call | flops 7247757312 | bytes 17301504 | tf_op jit(solution)/shard_map/ffn_first/pallas_call | solution.py:386
  63.3 17.3 %ffn_last.1 = (bf16[512,768]{1,0:T(8,128)(2,1)}, f32[512,768]{1,0:T(8,128)}, bf16[512,768]{1,0:T(8,128)(2,1)}, f32[1,768]{1,0:T(1,128)}, bf16[384,1024]{1,0:T(8,...) custom-call(s32[1]{0:T(128)} %bitcast.core_ref, ...), custom_call_target="tpu_custom_call" | custom-call | flops 7247757312 | bytes 17301504 | tf_op jit(solution)/shard_map/ffn_last/pallas_call | solution.py:403
  81.2 26.8 %attend_back.1 = (bf16[512,768]{1,0:T(8,128)(2,1)}, bf16[512,768]{1,0:T(8,128)(2,1)}, bf16[512,768]{1,0:T(8,128)(2,1)}, bf16[512,768]{1,0:T(8,128)(2,1)}, bf16[5...) custom-call(s32[1]{0:T(128)} %bitcast.core_ref, s32[2]{0:T(128)} %fusion.22.limits_ref, ...), custom_call_target="tpu_custom_call" | custom-call | flops 16106127360 | bytes 12582912 | tf_op jit(solution)/shard_map/attend_back/pallas_call | solution.py:255
  108.5 7.5 %project_grads.1 = (bf16[384,768]{1,0:T(8,128)(2,1)}, bf16[384,768]{1,0:T(8,128)(2,1)}, bf16[384,768]{1,0:T(8,128)(2,1)}, bf16[384,768]{1,0:T(8,128)(2,1)}, bf16...) custom-call(s32[1]{0:T(128)} %bitcast.core_ref, bf16[512,768]{1,0:T(8,128)(2,1)} %get-tuple-element.72.dq_ref, ...), custom_call_target="tpu_custom_call" | custom-call | flops 3019898880 | bytes 9043968 | tf_op jit(solution)/shard_map/project_grads/pallas_call | solution.py:437
  116.2 8.3 %project_back.1 = (f32[512,768]{1,0:T(8,128)}, bf16[512,768]{1,0:T(8,128)(2,1)}, f32[1,768]{1,0:T(1,128)}) custom-call(s32[1]{0:T(128)} %bitcast.core_ref, bf16[2,384]{1,0:T(2,128)(2,1)} %copy-done.22, bf16[2,384]{1,0:T(2,128)(2,1)} %copy-done.24, bf16[512,768]{1,0:T(8,128)(2,1)} %get-tuple-element.72.dq_ref, bf16[512,768]{1,0:T(8,128)(2,1)} %get-tuple-element.73.refs_0_, ...), custom_call_target="tpu_custom_call" | custom-call | flops 3019898880 | bytes 10616832 | tf_op jit(solution)/shard_map/project_back/pallas_call | solution.py:472
  125.3 40.9 %psum.7 = f32[2,768]{1,0:T(2,128)S(1)} all-reduce(f32[2,768]{1,0:T(2,128)S(1)} %pad_maximum_fusion.20), channel_id=1, replica_groups=mesh['grp'=8,'ctx'=2,'wsh'=2] {'grp','ctx','wsh'}, use_global_device_ids=true, to_apply=%region_0.1 | all-reduce | flops 1536 | bytes 12288 | tf_op jit(solution)/shard_map/psum | solution.py:620
  186.2 9.1 %collective-permute-done.9.refs_0_ = bf16[512,768]{1,0:T(8,128)(2,1)} collective-permute-done((bf16[512,768]{1,0:T(8,128)(2,1)S(1)}, bf16[512,768]{1,0:T(8,128)(2,1)}, u32[]{:S(2)}, u32[]{:S(2)}) %collective-permute-start.9) | collective-permute-done | bytes 786464 | tf_op jit(solution)/shard_map/ppermute | solution.py:515
  196.7 4.5 %input_grad.1 = bf16[512,768]{1,0:T(8,128)(2,1)} custom-call(s32[1]{0:T(128)} %bitcast.core_ref, bf16[2,384]{1,0:T(2,128)(2,1)} %copy-done.22, bf16[2,384]{1,0:T(2,128)(2,1)} %copy-done.24, bf16[512,768]{1,0:T(8,128)(2,1)} %bitcast.13, f32[512,768]{1,0:T(8,128)} %get-tuple-element.68.dm_ref, f32[512,768]{1,0:T(8,128)} %get-tuple-element.77.own_ref, ...), custom_call_target="tpu_custom_call" | custom-call | flops 393216 | bytes 6291456 | tf_op jit(solution)/shard_map/input_grad/pallas_call | solution.py:501
  214.5 15.0 %collective-permute-done.36 = bf16[96,768]{1,0:T(8,128)(2,1)S(1)} collective-permute-done((bf16[96,768]{1,0:T(8,128)(2,1)S(1)}, bf16[96,768]{1,0:T(8,128)(2,1)S(1)}, u32[]{:S(2)}, u32[]{:S(2)}) %collective-permute-start.36) | collective-permute-done | bytes 147488 | tf_op jit(solution)/shard_map/ppermute | solution.py:515
  231.0 3.7 collective-permute-done.12
  241.4 3.7 collective-permute-done.20
  294.4 4.1 collective-permute-done.51
  306.4 4.2 collective-permute-done.84
  328.8 5.9 %collective-permute-done.78 = bf16[64,768]{1,0:T(8,128)(2,1)S(1)} collective-permute-done((bf16[64,768]{1,0:T(8,128)(2,1)S(1)}, bf16[64,768]{1,0:T(8,128)(2,1)S(1)}, u32[]{:S(2)}, u32[]{:S(2)}) %collective-permute-start.78) | collective-permute-done | bytes 98336 | tf_op jit(solution)/shard_map/ppermute | solution.py:515
  334.7 5.9 %collective-permute-done.86 = bf16[64,768]{1,0:T(8,128)(2,1)S(1)} collective-permute-done((bf16[64,768]{1,0:T(8,128)(2,1)S(1)}, bf16[64,768]{1,0:T(8,128)(2,1)S(1)}, u32[]{:S(2)}, u32[]{:S(2)}) %collective-permute-start.86) | collective-permute-done | bytes 98336 | tf_op jit(solution)/shard_map/ppermute | solution.py:515
  340.7 5.5 %collective-permute-done.62 = bf16[48,1024]{1,0:T(8,128)(2,1)S(1)} collective-permute-done((bf16[48,1024]{1,0:T(8,128)(2,1)S(1)}, bf16[48,1024]{1,0:T(8,128)(2,1)S(1)}, u32[]{:S(2)}, u32[]{:S(2)}) %collective-permute-start.62) | collective-permute-done | bytes 98336 | tf_op jit(solution)/shard_map/ppermute | solution.py:515
  346.3 5.6 %collective-permute-done.70 = bf16[48,1024]{1,0:T(8,128)(2,1)S(1)} collective-permute-done((bf16[48,1024]{1,0:T(8,128)(2,1)S(1)}, bf16[48,1024]{1,0:T(8,128)(2,1)S(1)}, u32[]{:S(2)}, u32[]{:S(2)}) %collective-permute-start.70) | collective-permute-done | bytes 98336 | tf_op jit(solution)/shard_map/ppermute | solution.py:515
  351.9 5.9 %collective-permute-done.46 = bf16[48,1024]{1,0:T(8,128)(2,1)S(1)} collective-permute-done((bf16[48,1024]{1,0:T(8,128)(2,1)S(1)}, bf16[48,1024]{1,0:T(8,128)(2,1)S(1)}, u32[]{:S(2)}, u32[]{:S(2)}) %collective-permute-start.46) | collective-permute-done | bytes 98336 | tf_op jit(solution)/shard_map/ppermute | solution.py:515
  358.4 5.7 %collective-permute-done.54 = bf16[48,1024]{1,0:T(8,128)(2,1)S(1)} collective-permute-done((bf16[48,1024]{1,0:T(8,128)(2,1)S(1)}, bf16[48,1024]{1,0:T(8,128)(2,1)S(1)}, u32[]{:S(2)}, u32[]{:S(2)}) %collective-permute-start.54) | collective-permute-done | bytes 98336 | tf_op jit(solution)/shard_map/ppermute | solution.py:515
  364.1 5.1 %collective-permute-done.79 = bf16[64,768]{1,0:T(8,128)(2,1)S(1)} collective-permute-done((bf16[64,768]{1,0:T(8,128)(2,1)S(1)}, bf16[64,768]{1,0:T(8,128)(2,1)S(1)}, u32[]{:S(2)}, u32[]{:S(2)}) %collective-permute-start.79) | collective-permute-done | bytes 98336 | tf_op jit(solution)/shard_map/ppermute | solution.py:515
  369.9 5.1 %collective-permute-done.87 = bf16[64,768]{1,0:T(8,128)(2,1)S(1)} collective-permute-done((bf16[64,768]{1,0:T(8,128)(2,1)S(1)}, bf16[64,768]{1,0:T(8,128)(2,1)S(1)}, u32[]{:S(2)}, u32[]{:S(2)}) %collective-permute-start.87) | collective-permute-done | bytes 98336 | tf_op jit(solution)/shard_map/ppermute | solution.py:515
  375.2 5.5 %collective-permute-done.63 = bf16[48,1024]{1,0:T(8,128)(2,1)S(1)} collective-permute-done((bf16[48,1024]{1,0:T(8,128)(2,1)S(1)}, bf16[48,1024]{1,0:T(8,128)(2,1)S(1)}, u32[]{:S(2)}, u32[]{:S(2)}) %collective-permute-start.63) | collective-permute-done | bytes 98336 | tf_op jit(solution)/shard_map/ppermute | solution.py:515
  380.7 4.6 %collective-permute-done.71 = bf16[48,1024]{1,0:T(8,128)(2,1)S(1)} collective-permute-done((bf16[48,1024]{1,0:T(8,128)(2,1)S(1)}, bf16[48,1024]{1,0:T(8,128)(2,1)S(1)}, u32[]{:S(2)}, u32[]{:S(2)}) %collective-permute-start.71) | collective-permute-done | bytes 98336 | tf_op jit(solution)/shard_map/ppermute | solution.py:515
  385.5 4.4 %collective-permute-done.47 = bf16[48,1024]{1,0:T(8,128)(2,1)S(1)} collective-permute-done((bf16[48,1024]{1,0:T(8,128)(2,1)S(1)}, bf16[48,1024]{1,0:T(8,128)(2,1)S(1)}, u32[]{:S(2)}, u32[]{:S(2)}) %collective-permute-start.47) | collective-permute-done | bytes 98336 | tf_op jit(solution)/shard_map/ppermute | solution.py:515
  390.1 4.4 %collective-permute-done.55 = bf16[48,1024]{1,0:T(8,128)(2,1)S(1)} collective-permute-done((bf16[48,1024]{1,0:T(8,128)(2,1)S(1)}, bf16[48,1024]{1,0:T(8,128)(2,1)S(1)}, u32[]{:S(2)}, u32[]{:S(2)}) %collective-permute-start.55) | collective-permute-done | bytes 98336 | tf_op jit(solution)/shard_map/ppermute | solution.py:515
  410.8 5.2 %collective-permute-done.65 = bf16[192,1024]{1,0:T(8,128)(2,1)S(1)} collective-permute-done((bf16[192,1024]{1,0:T(8,128)(2,1)S(1)}, bf16[192,1024]{1,0:T(8,128)(2,1)S(1)}, u32[]{:S(2)}, u32[]{:S(2)}) %collective-permute-start.65) | collective-permute-done | bytes 393248 | tf_op jit(solution)/shard_map/ppermute | solution.py:515
  416.3 4.0 collective-permute-done.73
  (373 shorter events, 159.5 us)
Async XLA Ops:
  3.1 43.7 %collective-permute-start.6 = (bf16[384,2048]{1,0:T(8,128)(2,1)}, bf16[384,2048]{1,0:T(8,128)(2,1)S(1)}, u32[]{:S(2)}, u32[]{:S(2)}) collective-permute-start(bf16[384,2048]{1,0:T(8,128)(2,1)} %refs_0_.7), channel_id=1, source_target_pairs={{0,1},{1,0},{2,3},{3,2},{4,5},{5,4},{6,7},{7,6},{8,9},{9,8},{10,11... | collective-permute-start | bytes 4718600 | tf_op jit(solution)/shard_map/ppermute | solution.py:515
  3.2 43.7 %collective-permute-start.7 = (bf16[384,2048]{1,0:T(8,128)(2,1)}, bf16[384,2048]{1,0:T(8,128)(2,1)}, u32[]{:S(2)}, u32[]{:S(2)}) collective-permute-start(bf16[384,2048]{1,0:T(8,128)(2,1)} %refs_2_.7), channel_id=1, source_target_pairs={{0,1},{1,0},{2,3},{3,2},{4,5},{5,4},{6,7},{7,6},{8,9},{9,8},{10,11... | collective-permute-start | bytes 4718600 | tf_op jit(solution)/shard_map/ppermute | solution.py:515
  3.9 42.9 %collective-permute-start.8 = (bf16[1024,768]{1,0:T(8,128)(2,1)}, bf16[1024,768]{1,0:T(8,128)(2,1)}, u32[]{:S(2)}, u32[]{:S(2)}) collective-permute-start(bf16[1024,768]{1,0:T(8,128)(2,1)} %refs_4_.5), channel_id=1, source_target_pairs={{0,1},{1,0},{2,3},{3,2},{4,5},{5,4},{6,7},{7,6},{8,9},{9,8},{10,11... | collective-permute-start | bytes 4718600 | tf_op jit(solution)/shard_map/ppermute | solution.py:515
  4.3 20.9 %collective-permute-start.4 = (bf16[512,768]{1,0:T(8,128)(2,1)}, bf16[512,768]{1,0:T(8,128)(2,1)S(1)}, u32[]{:S(2)}, u32[]{:S(2)}) collective-permute-start(bf16[512,768]{1,0:T(8,128)(2,1)} %bitcast.9), channel_id=1, source_target_pairs={{0,2},{2,0},{1,3},{3,1},{4,6},{6,4},{5,7},{7,5},{8,10},{10,8},{9,1... | collective-permute-start | bytes 2359304 | tf_op jit(solution)/shard_map/ppermute | solution.py:515
  12.2 34.6 %collective-permute-start.5 = (bf16[384,768]{1,0:T(8,128)(2,1)}, bf16[384,768]{1,0:T(8,128)(2,1)}, u32[]{:S(2)}, u32[]{:S(2)}) collective-permute-start(bf16[384,768]{1,0:T(8,128)(2,1)} %refs_8_.2), channel_id=1, source_target_pairs={{0,1},{1,0},{2,3},{3,2},{4,5},{5,4},{6,7},{7,6},{8,9},{9,8},{10,11... | collective-permute-start | bytes 1769480 | tf_op jit(solution)/shard_map/ppermute | solution.py:515
  63.2 109.7 %collective-permute-start.74 = (bf16[512,768]{1,0:T(8,128)(2,1)}, bf16[512,768]{1,0:T(8,128)(2,1)S(1)}, u32[]{:S(2)}, u32[]{:S(2)}) collective-permute-start(bf16[512,768]{1,0:T(8,128)(2,1)} %get-tuple-element.98), channel_id=1, source_target_pairs={{0,1},{1,0},{2,3},{3,2},{4,5},{5,4},{6,7},{7,6},{8,9},{9,8},{10,11... | collective-permute-start | bytes 2359304 | tf_op jit(solution)/shard_map/ppermute | solution.py:515
  80.6 93.8 %collective-permute-start.82 = (bf16[512,768]{1,0:T(8,128)(2,1)}, bf16[512,768]{1,0:T(8,128)(2,1)S(1)}, u32[]{:S(2)}, u32[]{:S(2)}) collective-permute-start(bf16[512,768]{1,0:T(8,128)(2,1)} %get-tuple-element.100), channel_id=1, source_target_pairs={{0,1},{1,0},{2,3},{3,2},{4,5},{5,4},{6,7},{7,6},{8,9},{9,8},{10,11... | collective-permute-start | bytes 2359304 | tf_op jit(solution)/shard_map/ppermute | solution.py:515
  81.1 95.9 %collective-permute-start.58 = (bf16[384,1024]{1,0:T(8,128)(2,1)}, bf16[384,1024]{1,0:T(8,128)(2,1)}, u32[]{:S(2)}, u32[]{:S(2)}) collective-permute-start(bf16[384,1024]{1,0:T(8,128)(2,1)} %get-tuple-element.94), channel_id=1, source_target_pairs={{0,1},{1,0},{2,3},{3,2},{4,5},{5,4},{6,7},{7,6},{8,9},{9,8},{10,11... | collective-permute-start | bytes 2359304 | tf_op jit(solution)/shard_map/ppermute | solution.py:515
  108.0 58.9 %collective-permute-start.34 = (bf16[384,768]{1,0:T(8,128)(2,1)}, bf16[384,768]{1,0:T(8,128)(2,1)S(1)}, u32[]{:S(2)}, u32[]{:S(2)}) collective-permute-start(bf16[384,768]{1,0:T(8,128)(2,1)} %get-tuple-element.88), channel_id=1, source_target_pairs={{0,1},{1,0},{2,3},{3,2},{4,5},{5,4},{6,7},{7,6},{8,9},{9,8},{10,11... | collective-permute-start | bytes 1769480 | tf_op jit(solution)/shard_map/ppermute | solution.py:515
  116.0 51.0 %collective-permute-start.10 = (bf16[384,768]{1,0:T(8,128)(2,1)}, bf16[384,768]{1,0:T(8,128)(2,1)}, u32[]{:S(2)}, u32[]{:S(2)}) collective-permute-start(bf16[384,768]{1,0:T(8,128)(2,1)} %get-tuple-element.82), channel_id=1, source_target_pairs={{0,1},{1,0},{2,3},{3,2},{4,5},{5,4},{6,7},{7,6},{8,9},{9,8},{10,11... | collective-permute-start | bytes 1769480 | tf_op jit(solution)/shard_map/ppermute | solution.py:515
  172.9 11.4 %collective-permute-start.50 = (bf16[384,1024]{1,0:T(8,128)(2,1)S(1)}, bf16[384,1024]{1,0:T(8,128)(2,1)S(1)}, u32[]{:S(2)}, u32[]{:S(2)}) collective-permute-start(bf16[384,1024]{1,0:T(8,128)(2,1)S(1)} %copy-done.28), channel_id=1, source_target_pairs={{0,1},{1,0},{2,3},{3,2},{4,5},{5,4},{6,7},{7,6},{8,9},{9,8},{10,11... | collective-permute-start | bytes 2359304 | tf_op jit(solution)/shard_map/ppermute | solution.py:515
  174.5 20.7 %collective-permute-start.9 = (bf16[512,768]{1,0:T(8,128)(2,1)S(1)}, bf16[512,768]{1,0:T(8,128)(2,1)}, u32[]{:S(2)}, u32[]{:S(2)}) collective-permute-start(bf16[512,768]{1,0:T(8,128)(2,1)S(1)} %copy-done.30), channel_id=1, source_target_pairs={{0,2},{2,0},{1,3},{3,1},{4,6},{6,4},{5,7},{7,5},{8,10},{10,8},{9,1... | collective-permute-start | bytes 2359304 | tf_op jit(solution)/shard_map/ppermute | solution.py:515
  177.0 24.5 %collective-permute-start.35 = (bf16[192,768]{1,0:T(8,128)(2,1)}, bf16[192,768]{1,0:T(8,128)(2,1)}, u32[]{:S(2)}, u32[]{:S(2)}) collective-permute-start(bf16[192,768]{1,0:T(8,128)(2,1)} %constant_dynamic-slice_fusion.21), channel_id=1, source_target_pairs={{0,2},{2,0},{1,3},{3,1},{4,6},{6,4},{5,7},{7,5},{8,10},{10,8},{9,1... | collective-permute-start | bytes 884744 | tf_op jit(solution)/shard_map/ppermute | solution.py:515
  180.0 30.1 %collective-permute-start.27 = (bf16[192,768]{1,0:T(8,128)(2,1)}, bf16[192,768]{1,0:T(8,128)(2,1)}, u32[]{:S(2)}, u32[]{:S(2)}) collective-permute-start(bf16[192,768]{1,0:T(8,128)(2,1)} %constant_dynamic-slice_fusion.24), channel_id=1, source_target_pairs={{0,8},{4,12},{8,0},{12,4},{16,24},{20,28},{24,16},{28,20},{1,9},{5... | collective-permute-start | bytes 884744 | tf_op jit(solution)/shard_map/ppermute | solution.py:515
  182.7 28.9 %collective-permute-start.19 = (bf16[192,768]{1,0:T(8,128)(2,1)}, bf16[192,768]{1,0:T(8,128)(2,1)}, u32[]{:S(2)}, u32[]{:S(2)}) collective-permute-start(bf16[192,768]{1,0:T(8,128)(2,1)} %constant_dynamic-slice_fusion.27), channel_id=1, source_target_pairs={{0,4},{4,0},{8,12},{12,8},{16,20},{20,16},{24,28},{28,24},{1,5},{5... | collective-permute-start | bytes 884744 | tf_op jit(solution)/shard_map/ppermute | solution.py:515
  184.4 23.0 %collective-permute-start.11 = (bf16[192,768]{1,0:T(8,128)(2,1)}, bf16[192,768]{1,0:T(8,128)(2,1)}, u32[]{:S(2)}, u32[]{:S(2)}) collective-permute-start(bf16[192,768]{1,0:T(8,128)(2,1)} %constant_dynamic-slice_fusion.30), channel_id=1, source_target_pairs={{0,2},{2,0},{1,3},{3,1},{4,6},{6,4},{5,7},{7,5},{8,10},{10,8},{9,1... | collective-permute-start | bytes 884744 | tf_op jit(solution)/shard_map/ppermute | solution.py:515
  195.2 89.6 %collective-permute-start.75 = (bf16[256,768]{1,0:T(8,128)(2,1)}, bf16[256,768]{1,0:T(8,128)(2,1)}, u32[]{:S(2)}, u32[]{:S(2)}) collective-permute-start(bf16[256,768]{1,0:T(8,128)(2,1)} %constant_dynamic-slice_fusion.6), channel_id=1, source_target_pairs={{0,8},{4,12},{8,0},{12,4},{16,24},{20,28},{24,16},{28,20},{1,9},{5... | collective-permute-start | bytes 1179656 | tf_op jit(solution)/shard_map/ppermute | solution.py:515
  201.6 85.5 %collective-permute-start.83 = (bf16[256,768]{1,0:T(8,128)(2,1)}, bf16[256,768]{1,0:T(8,128)(2,1)S(1)}, u32[]{:S(2)}, u32[]{:S(2)}) collective-permute-start(bf16[256,768]{1,0:T(8,128)(2,1)} %constant_dynamic-slice_fusion.3), channel_id=1, source_target_pairs={{0,8},{4,12},{8,0},{12,4},{16,24},{20,28},{24,16},{28,20},{1,9},{5... | collective-permute-start | bytes 1179656 | tf_op jit(solution)/shard_map/ppermute | solution.py:515
  207.3 81.3 %collective-permute-start.59 = (bf16[192,1024]{1,0:T(8,128)(2,1)S(1)}, bf16[192,1024]{1,0:T(8,128)(2,1)S(1)}, u32[]{:S(2)}, u32[]{:S(2)}) collective-permute-start(bf16[192,1024]{1,0:T(8,128)(2,1)S(1)} %copy-done.20), channel_id=1, source_target_pairs={{0,4},{4,0},{8,12},{12,8},{16,20},{20,16},{24,28},{28,24},{1,5},{5... | collective-permute-start | bytes 1179656 | tf_op jit(solution)/shard_map/ppermute | solution.py:515
  210.2 79.8 %collective-permute-start.67 = (bf16[192,1024]{1,0:T(8,128)(2,1)S(1)}, bf16[192,1024]{1,0:T(8,128)(2,1)S(1)}, u32[]{:S(2)}, u32[]{:S(2)}) collective-permute-start(bf16[192,1024]{1,0:T(8,128)(2,1)S(1)} %copy-done.21), channel_id=1, source_target_pairs={{0,4},{4,0},{8,12},{12,8},{16,20},{20,16},{24,28},{28,24},{1,5},{5... | collective-permute-start | bytes 1179656 | tf_op jit(solution)/shard_map/ppermute | solution.py:515
  211.6 17.9 %collective-permute-start.36 = (bf16[96,768]{1,0:T(8,128)(2,1)S(1)}, bf16[96,768]{1,0:T(8,128)(2,1)S(1)}, u32[]{:S(2)}, u32[]{:S(2)}) collective-permute-start(bf16[96,768]{1,0:T(8,128)(2,1)S(1)} %constant_dynamic-slice_fusion.20), channel_id=1, source_target_pairs={{0,4},{4,0},{8,12},{12,8},{16,20},{20,16},{24,28},{28,24},{1,5},{5... | collective-permute-start | bytes 442376 | tf_op jit(solution)/shard_map/ppermute | solution.py:515
  284.8 13.7 %collective-permute-start.51 = (bf16[192,1024]{1,0:T(8,128)(2,1)S(1)}, bf16[192,1024]{1,0:T(8,128)(2,1)S(1)}, u32[]{:S(2)}, u32[]{:S(2)}) collective-permute-start(bf16[192,1024]{1,0:T(8,128)(2,1)S(1)} %constant_dynamic-slice_fusion.15), channel_id=1, source_target_pairs={{0,2},{2,0},{1,3},{3,1},{4,6},{6,4},{5,7},{7,5},{8,10},{10,8},{9,1... | collective-permute-start | bytes 1179656 | tf_op jit(solution)/shard_map/ppermute | solution.py:515
  287.1 12.1 %collective-permute-start.39 = (bf16[48,768]{1,0:T(8,128)(2,1)S(1)}, bf16[48,768]{1,0:T(8,128)(2,1)S(1)}, u32[]{:S(2)}, u32[]{:S(2)}) collective-permute-start(bf16[48,768]{1,0:T(8,128)(2,1)S(1)} %add_convert_fusion.42), channel_id=1, source_target_pairs={{0,8},{4,12},{8,0},{12,4},{16,24},{20,28},{24,16},{28,20},{1,9},{5... | collective-permute-start | bytes 221192 | tf_op jit(solution)/shard_map/ppermute | solution.py:515
  288.6 13.7 %collective-permute-start.31 = (bf16[48,768]{1,0:T(8,128)(2,1)S(1)}, bf16[48,768]{1,0:T(8,128)(2,1)S(1)}, u32[]{:S(2)}, u32[]{:S(2)}) collective-permute-start(bf16[48,768]{1,0:T(8,128)(2,1)S(1)} %add_convert_fusion.44), channel_id=1, source_target_pairs={{0,4},{4,0},{8,12},{12,8},{16,20},{20,16},{24,28},{28,24},{1,5},{5... | collective-permute-start | bytes 221192 | tf_op jit(solution)/shard_map/ppermute | solution.py:515
  290.0 13.0 %collective-permute-start.23 = (bf16[48,768]{1,0:T(8,128)(2,1)S(1)}, bf16[48,768]{1,0:T(8,128)(2,1)S(1)}, u32[]{:S(2)}, u32[]{:S(2)}) collective-permute-start(bf16[48,768]{1,0:T(8,128)(2,1)S(1)} %add_convert_fusion.46), channel_id=1, source_target_pairs={{0,2},{2,0},{1,3},{3,1},{4,6},{6,4},{5,7},{7,5},{8,10},{10,8},{9,1... | collective-permute-start | bytes 221192 | tf_op jit(solution)/shard_map/ppermute | solution.py:515
  322.4 72.1 %collective-permute-start.41 = (bf16[192,768]{1,0:T(8,128)(2,1)S(1)}, bf16[192,768]{1,0:T(8,128)(2,1)S(1)}, u32[]{:S(2)}, u32[]{:S(2)}) collective-permute-start(bf16[192,768]{1,0:T(8,128)(2,1)S(1)} %pad_maximum_fusion.9), channel_id=1, source_target_pairs={{0,2},{2,0},{1,3},{3,1},{4,6},{6,4},{5,7},{7,5},{8,10},{10,8},{9,1... | collective-permute-start | bytes 884744 | tf_op jit(solution)/shard_map/ppermute | solution.py:515
  323.6 73.1 %collective-permute-start.33 = (bf16[192,768]{1,0:T(8,128)(2,1)S(1)}, bf16[192,768]{1,0:T(8,128)(2,1)S(1)}, u32[]{:S(2)}, u32[]{:S(2)}) collective-permute-start(bf16[192,768]{1,0:T(8,128)(2,1)S(1)} %pad_maximum_fusion.8), channel_id=1, source_target_pairs={{0,8},{4,12},{8,0},{12,4},{16,24},{20,28},{24,16},{28,20},{1,9},{5... | collective-permute-start | bytes 884744 | tf_op jit(solution)/shard_map/ppermute | solution.py:515
  324.4 74.9 %collective-permute-start.25 = (bf16[192,768]{1,0:T(8,128)(2,1)S(1)}, bf16[192,768]{1,0:T(8,128)(2,1)S(1)}, u32[]{:S(2)}, u32[]{:S(2)}) collective-permute-start(bf16[192,768]{1,0:T(8,128)(2,1)S(1)} %pad_maximum_fusion.7), channel_id=1, source_target_pairs={{0,4},{4,0},{8,12},{12,8},{16,20},{20,16},{24,28},{28,24},{1,5},{5... | collective-permute-start | bytes 884744 | tf_op jit(solution)/shard_map/ppermute | solution.py:515
  326.2 75.1 %collective-permute-start.17 = (bf16[192,768]{1,0:T(8,128)(2,1)S(1)}, bf16[192,768]{1,0:T(8,128)(2,1)S(1)}, u32[]{:S(2)}, u32[]{:S(2)}) collective-permute-start(bf16[192,768]{1,0:T(8,128)(2,1)S(1)} %pad_maximum_fusion.6), channel_id=1, source_target_pairs={{0,2},{2,0},{1,3},{3,1},{4,6},{6,4},{5,7},{7,5},{8,10},{10,8},{9,1... | collective-permute-start | bytes 884744 | tf_op jit(solution)/shard_map/ppermute | solution.py:515
  405.8 21.8 %collective-permute-start.81 = (bf16[256,768]{1,0:T(8,128)(2,1)S(1)}, bf16[256,768]{1,0:T(8,128)(2,1)S(1)}, u32[]{:S(2)}, u32[]{:S(2)}) collective-permute-start(bf16[256,768]{1,0:T(8,128)(2,1)S(1)} %pad_maximum_fusion.4), channel_id=1, source_target_pairs={{0,8},{4,12},{8,0},{12,4},{16,24},{20,28},{24,16},{28,20},{1,9},{5... | collective-permute-start | bytes 1179656 | tf_op jit(solution)/shard_map/ppermute | solution.py:515
  406.1 24.8 %collective-permute-start.89 = (bf16[256,768]{1,0:T(8,128)(2,1)S(1)}, bf16[256,768]{1,0:T(8,128)(2,1)S(1)}, u32[]{:S(2)}, u32[]{:S(2)}) collective-permute-start(bf16[256,768]{1,0:T(8,128)(2,1)S(1)} %pad_maximum_fusion.5), channel_id=1, source_target_pairs={{0,8},{4,12},{8,0},{12,4},{16,24},{20,28},{24,16},{28,20},{1,9},{5... | collective-permute-start | bytes 1179656 | tf_op jit(solution)/shard_map/ppermute | solution.py:515
  408.5 11.7 %collective-permute-start.73 = (bf16[192,1024]{1,0:T(8,128)(2,1)S(1)}, bf16[192,1024]{1,0:T(8,128)(2,1)S(1)}, u32[]{:S(2)}, u32[]{:S(2)}) collective-permute-start(bf16[192,1024]{1,0:T(8,128)(2,1)S(1)} %pad_maximum_fusion.3), channel_id=1, source_target_pairs={{0,4},{4,0},{8,12},{12,8},{16,20},{20,16},{24,28},{28,24},{1,5},{5... | collective-permute-start | bytes 1179656 | tf_op jit(solution)/shard_map/ppermute | solution.py:515
  (92 other events, 661.8 us)
